TPU v7x, 32 devices: a whole 2x2x4 slice. The times are simulated.
32 devices in a mesh: grp: 2 (over x), lon: 8 (over z, y), lat: 2 (over core).
Axes of the slice: x: 2, y: 2, z: 4, core: 2. Of those that a mesh axis runs over, the one named last changes fastest.
Arguments:
- cloud_state: float32 [4, 256, 128, 1024], P('grp', 'lon', 'lat'), parts along dimension 0, may hold values from -6 to 6
- counts: int32 [512, 128], P(('grp', 'lon'), 'lat'), parts along dimension 0, may hold values from 1 to 8, as said below
- courant: float32 [32], replicated, may hold values from 0.2 to 0.9
- truncation: int32 [96], replicated, may hold values from 0 to 94, as said below
Outputs:
- cloud_next: float32 [4, 256, 128, 1024], P('grp', 'lon', 'lat'), parts along dimension 0
There are 2 independent parts, one for each index of `grp`. A program takes and returns all parts, laid end to end along the dimension named above; an argument that names none is the same for every part. Nothing has to cross between parts.
Inputs may be any that keep to these rules, and one draw needn't show every extreme that they name: `counts`: columns come in busy regions of 4 to 8 substeps and calm ones of 1 or 2; column 0, 0 has 8. truncation[m] lies in m .. 85 for m <= 85, truncation[0] = 85, and truncation[m] = m - 1 (nothing kept) for m > 85.
All inputs are finite; a program needn't handle non-finite values.
Results may differ from a plain program's by a relative error of at most 0.0003.
Values sent between devices are 32-bit elements; how exact they have to be, the bound alone decides.
No kernel may reach another device: no remote copies, remote signals or barrier semaphores. Data moves between devices by JAX's collectives and lax.ppermute only.
A program may use at most 64 MiB of HBM per device.

v0:
```python
import jax
import jax.numpy as jnp
from jax import lax
from jax.sharding import PartitionSpec as P

NN = 96


couple_gain = 8.0


def legendre(orders, lat_rows, lat_total, degrees):
    latitude = -0.5 * jnp.pi + jnp.pi * (lat_rows.astype(jnp.float32) + 0.5) / lat_total
    sin_lat = jnp.sin(latitude)
    cos_lat = jnp.cos(latitude)
    order_f = orders.astype(jnp.float32)
    ladder = jnp.arange(1, degrees + 1).astype(jnp.float32)
    log_gains = 0.5 * jnp.log((2.0 * ladder + 1.0) / (2.0 * ladder))
    included = (ladder[None, :] <= order_f[:, None]).astype(jnp.float32)
    log_start = 0.5 * jnp.log(jnp.float32(0.5)) + jnp.sum(included * log_gains[None, :], axis=1)
    diagonal = jnp.exp(log_start[:, None] + order_f[:, None] * jnp.log(cos_lat)[None, :])

    def legendre_advance(carry, degree):
        previous, earlier, inverse = carry
        degree_f = degree.astype(jnp.float32)
        higher = degree_f > order_f
        numerator = jnp.maximum(4.0 * degree_f * degree_f - 1.0, 1.0)
        denominator = jnp.where(higher, degree_f * degree_f - order_f * order_f, 1.0)
        factor = jnp.sqrt(numerator / denominator)
        raised = factor[:, None] * (sin_lat[None, :] * previous - inverse[:, None] * earlier)
        current = jnp.where(
            (degree_f == order_f)[:, None], diagonal, jnp.where(higher[:, None], raised, 0.0)
        )
        return ((current, previous, jnp.where(higher, 1.0 / factor, 0.0)), current)

    initial = (jnp.zeros_like(diagonal), jnp.zeros_like(diagonal), jnp.zeros_like(order_f))
    _, stacked = lax.scan(legendre_advance, initial, jnp.arange(degrees, dtype=jnp.int32), unroll=8)
    return jnp.transpose(stacked, (1, 0, 2))


def latitude_weights(lat_rows, lat_total):
    latitude = -0.5 * jnp.pi + jnp.pi * (lat_rows.astype(jnp.float32) + 0.5) / lat_total
    return jnp.pi * jnp.cos(latitude) / lat_total


def wave_table(lon_rows, modes, lon_total):
    phase = lon_rows[:, None] * modes[None, :] % lon_total
    angle = phase.astype(jnp.float32) * (2.0 * jnp.pi / lon_total)
    return (jnp.cos(angle), jnp.sin(angle))


def substep(theta, moist, force, count, index, rate, profile, levels):
    heated = theta + couple_gain * profile[None, None, :] * force[:, :, None]
    moved_theta = heated - rate * (heated - jnp.roll(heated, levels, axis=2))
    moved_moist = moist - rate * (moist - jnp.roll(moist, levels, axis=2))
    excess = moved_moist - (1.0 + 0.2 * moved_theta)
    condensed = 0.25 * (excess + jnp.sqrt(excess * excess + 0.01))
    active = (index < count)[:, :, None]
    return (
        jnp.where(active, moved_theta + 0.5 * condensed, theta),
        jnp.where(active, moved_moist - condensed, moist),
    )


def run_block(block_state, force_rows, count_rows, rate, profile, levels, trip_count):

    def unfinished(carry):
        return carry[0] < trip_count

    def run_advance(carry):
        index, theta, moist = carry
        theta, moist = substep(theta, moist, force_rows, count_rows, index, rate, profile, levels)
        return (index + 1, theta, moist)

    _, theta, moist = lax.while_loop(
        unfinished, run_advance, (jnp.int32(0), block_state[0], block_state[1])
    )
    return jnp.stack([theta, moist])


def shards(cloud_state, counts, courant, truncation):
    highest = lax.Precision.HIGHEST
    lon_devices = lax.axis_size("lon")
    lon_index = lax.axis_index("lon")
    lat_index = lax.axis_index("lat")
    fields, lon_local, lat_local, cells = cloud_state.shape
    levels = courant.shape[0]
    columns_across = cells // levels
    total_lon = lon_local * lon_devices
    total_lat = lat_local * lax.axis_size("lat")
    total_modes = truncation.shape[0]
    mode_local = total_modes // lon_devices
    heating = jnp.mean(cloud_state[0], axis=2)
    my_lons = lon_index * lon_local + jnp.arange(lon_local, dtype=jnp.int32)
    modes = jnp.arange(mode_local * lax.axis_size("lon"), dtype=jnp.int32)
    cosine_table, sine_table = wave_table(my_lons, modes, total_lon)
    coefs = lax.psum_scatter(
        jnp.stack(
            [
                jnp.dot(cosine_table.T, heating, precision=highest),
                jnp.dot(sine_table.T, heating, precision=highest),
            ],
            1,
        )
        / total_lon,
        "lon",
        scatter_dimension=0,
        tiled=True,
    )
    my_modes = lon_index * mode_local + jnp.arange(mode_local, dtype=jnp.int32)
    my_lats = lat_index * lat_local + jnp.arange(lat_local, dtype=jnp.int32)
    table = legendre(my_modes, my_lats, total_lat, NN)
    weights = latitude_weights(my_lats, total_lat)
    partial_spec = jnp.einsum(
        "mnj,mcj->mcn", table, coefs * weights[None, None, :], precision=highest
    )
    spectrum = lax.psum(partial_spec, "lat")
    my_trunc = lax.dynamic_slice_in_dim(truncation, lon_index * mode_local, mode_local)
    degrees = jnp.arange(NN, dtype=jnp.int32)
    keep_mask = (
        (degrees[None, :] >= my_modes[:, None]) & (degrees[None, :] <= my_trunc[:, None])
    ).astype(jnp.float32)
    filtered = jnp.einsum(
        "mnj,mcn->mcj", table, spectrum * keep_mask[:, None, :], precision=highest
    )
    piece = lax.all_gather(filtered, "lon", axis=0, tiled=True)
    modes = jnp.arange(piece.shape[0], dtype=jnp.int32)
    cosine_table, sine_table = wave_table(my_lons, modes, total_lon)
    factor = jnp.where(modes == 0, 1.0, 2.0).astype(jnp.float32)[:, None]
    forcing = jnp.dot(cosine_table, factor * piece[:, 0], precision=highest) + jnp.dot(
        sine_table, factor * piece[:, 1], precision=highest
    )
    level_profile = jnp.sin(jnp.pi * (jnp.arange(levels).astype(jnp.float32) + 0.5) / levels)
    profile = jnp.tile(level_profile, columns_across)
    rate = jnp.tile(courant, columns_across)[None, None, :]
    blocks_count = 8
    block_rows = lon_local // blocks_count
    block_cost = jnp.max(counts.reshape(blocks_count, block_rows, lat_local), axis=(1, 2))

    def visit(block_index, updated):
        start = block_index * block_rows
        piece = lax.dynamic_slice_in_dim(cloud_state, start, block_rows, 1)
        force_rows = lax.dynamic_slice_in_dim(forcing, start, block_rows, 0)
        count_rows = lax.dynamic_slice_in_dim(counts, start, block_rows, 0)
        result = run_block(
            piece, force_rows, count_rows, rate, profile, levels, block_cost[block_index]
        )
        return lax.dynamic_update_slice_in_dim(updated, result, start, 1)

    updated = lax.fori_loop(0, blocks_count, visit, cloud_state)
    return updated


def solution(mesh):
    return jax.shard_map(
        shards,
        mesh=mesh,
        in_specs=(P("grp", "lon", "lat", None), P(("grp", "lon"), "lat"), P(), P()),
        out_specs=P("grp", "lon", "lat", None),
        check_vma=False,
    )
```

profile of v0, /device:TPU:18, one launch (start us, length us, event | category | flops | bytes accessed | tf_op | source)
XLA Modules:
  0.0 382.6 jit_solution(14909525809693610050)
XLA Ops:
  4.3 3.8 slice_reduce_fusion
  8.8 33.5 %all-reduce = f32[96,2,64]{2,1,0:T(2,128)S(1)} all-reduce(f32[96,2,64]{2,1,0:T(2,128)S(1)} %copy.12), channel_id=2, replica_groups=mesh['grp'=2,'lon'=8,'lat'=2] {'lon'}, use_global_device_ids=true, to_apply=%region_1.2.clone | all-reduce | flops 12288 | bytes 98304
  42.4 82.5 %while.81 = (s32[]{:T(128)}, f32[12,64]{1,0:T(8,128)S(1)}, f32[12,64]{1,0:T(8,128)S(1)}, f32[12]{0:T(128)S(1)}, f32[12,8,12,64]{3,2,1,0:T(8,128)S(1)}, /*index=5...) while((s32[]{:T(128)}, f32[12,64]{1,0:T(8,128)S(1)}, ...), condition=%wide.region_4.5_spmd.clone.clone.clone, body=%wide.region_3.4_spmd.clone.clone.clone.sunk | while | flops 108922 | bytes 421596 | solution.py:37
  125.6 3.3 psum.7
  129.6 30.6 %all_gather.3 = f32[96,2,64]{2,1,0:T(2,128)S(1)} all-gather(f32[12,2,64]{2,1,0:T(2,128)S(1)} %fusion.42), channel_id=1, replica_groups=mesh['grp'=2,'lon'=8,'lat'=2] {'lon'}, dimensions={0}, use_global_device_ids=true | all-gather | bytes 55296 | tf_op jit(solution)/shard_map/all_gather | solution.py:126
  160.9 12.0 %copy.50 = f32[2,32,64,1024]{3,2,1,0:T(8,128)} copy(f32[2,32,64,1024]{3,2,1,0:T(8,128)} %param.10) | data formatting | bytes 33554432
  172.9 209.7 %while.80 = (s32[]{:T(128)}, f32[2,32,64,1024]{3,2,1,0:T(8,128)}, f32[2,32,64,1024]{3,2,1,0:T(8,128)}, s32[8]{0:T(128)S(1)}, f32[32,64]{1,0:T(8,128)S(1)}, /*ind...) while((s32[]{:T(128)}, f32[2,32,64,1024]{3,2,1,0:T(8,128)}, ...), condition=%wide.region_11.12_spmd.clone, body=%wide.region_8.11_spmd.clone.sunk | while | flops 6817033 | bytes 18993312 | solution.py:150
  174.3 1.7 dynamic-slice_bitcast_fusion.3
  175.9 21.7 %while.82 = (s32[]{:T(128)}, f32[4,64,1024]{2,1,0:T(8,128)S(1)}, f32[4,64,1024]{2,1,0:T(8,128)S(1)}, s32[]{:T(128)}, s32[4,64]{1,0:T(4,128)S(1)}, /*index=5*/f32...) while((s32[]{:T(128)}, f32[4,64,1024]{2,1,0:T(8,128)S(1)}, ...), condition=%wide.region_10.10_spmd, body=%wide.region_9.9_spmd.sunk | while | flops 6292738 | bytes 10583657 | solution.py:75
  179.8 1.4 subtract_select_fusion.2
  182.4 1.4 subtract_select_fusion.2
  185.0 1.4 subtract_select_fusion.2
  190.3 1.4 subtract_select_fusion.2
  192.9 1.4 subtract_select_fusion.2
  195.6 1.4 subtract_select_fusion.2
  197.6 1.5 maximum_dynamic-update-slice_fusion.2
  200.5 1.7 dynamic-slice_bitcast_fusion.3
  202.2 21.7 %while.82 = (s32[]{:T(128)}, f32[4,64,1024]{2,1,0:T(8,128)S(1)}, f32[4,64,1024]{2,1,0:T(8,128)S(1)}, s32[]{:T(128)}, s32[4,64]{1,0:T(4,128)S(1)}, /*index=5*/f32...) while((s32[]{:T(128)}, f32[4,64,1024]{2,1,0:T(8,128)S(1)}, ...), condition=%wide.region_10.10_spmd, body=%wide.region_9.9_spmd.sunk | while | flops 6292738 | bytes 10583657 | solution.py:75
  203.4 1.4 subtract_select_fusion.2
  206.0 1.4 subtract_select_fusion.2
  208.6 1.4 subtract_select_fusion.2
  211.3 1.4 subtract_select_fusion.2
  216.5 1.4 subtract_select_fusion.2
  219.2 1.4 subtract_select_fusion.2
  221.8 1.4 subtract_select_fusion.2
  223.9 1.5 maximum_dynamic-update-slice_fusion.2
  226.7 1.7 dynamic-slice_bitcast_fusion.3
  228.4 21.7 %while.82 = (s32[]{:T(128)}, f32[4,64,1024]{2,1,0:T(8,128)S(1)}, f32[4,64,1024]{2,1,0:T(8,128)S(1)}, s32[]{:T(128)}, s32[4,64]{1,0:T(4,128)S(1)}, /*index=5*/f32...) while((s32[]{:T(128)}, f32[4,64,1024]{2,1,0:T(8,128)S(1)}, ...), condition=%wide.region_10.10_spmd, body=%wide.region_9.9_spmd.sunk | while | flops 6292738 | bytes 10583657 | solution.py:75
  229.6 1.4 subtract_select_fusion.2
  232.2 1.4 subtract_select_fusion.2
  234.8 1.4 subtract_select_fusion.2
  240.1 1.4 subtract_select_fusion.2
  250.1 1.5 maximum_dynamic-update-slice_fusion.2
  252.9 1.7 dynamic-slice_bitcast_fusion.3
  254.6 21.7 %while.82 = (s32[]{:T(128)}, f32[4,64,1024]{2,1,0:T(8,128)S(1)}, f32[4,64,1024]{2,1,0:T(8,128)S(1)}, s32[]{:T(128)}, s32[4,64]{1,0:T(4,128)S(1)}, /*index=5*/f32...) while((s32[]{:T(128)}, f32[4,64,1024]{2,1,0:T(8,128)S(1)}, ...), condition=%wide.region_10.10_spmd, body=%wide.region_9.9_spmd.sunk | while | flops 6292738 | bytes 10583657 | solution.py:75
  276.3 1.5 maximum_dynamic-update-slice_fusion.2
  279.1 1.7 dynamic-slice_bitcast_fusion.3
  280.8 21.7 %while.82 = (s32[]{:T(128)}, f32[4,64,1024]{2,1,0:T(8,128)S(1)}, f32[4,64,1024]{2,1,0:T(8,128)S(1)}, s32[]{:T(128)}, s32[4,64]{1,0:T(4,128)S(1)}, /*index=5*/f32...) while((s32[]{:T(128)}, f32[4,64,1024]{2,1,0:T(8,128)S(1)}, ...), condition=%wide.region_10.10_spmd, body=%wide.region_9.9_spmd.sunk | while | flops 6292738 | bytes 10583657 | solution.py:75
  302.5 1.5 maximum_dynamic-update-slice_fusion.2
  305.4 1.7 dynamic-slice_bitcast_fusion.3
  307.0 21.7 %while.82 = (s32[]{:T(128)}, f32[4,64,1024]{2,1,0:T(8,128)S(1)}, f32[4,64,1024]{2,1,0:T(8,128)S(1)}, s32[]{:T(128)}, s32[4,64]{1,0:T(4,128)S(1)}, /*index=5*/f32...) while((s32[]{:T(128)}, f32[4,64,1024]{2,1,0:T(8,128)S(1)}, ...), condition=%wide.region_10.10_spmd, body=%wide.region_9.9_spmd.sunk | while | flops 6292738 | bytes 10583657 | solution.py:75
  328.7 1.5 maximum_dynamic-update-slice_fusion.2
  331.6 1.7 dynamic-slice_bitcast_fusion.3
  333.2 21.7 %while.82 = (s32[]{:T(128)}, f32[4,64,1024]{2,1,0:T(8,128)S(1)}, f32[4,64,1024]{2,1,0:T(8,128)S(1)}, s32[]{:T(128)}, s32[4,64]{1,0:T(4,128)S(1)}, /*index=5*/f32...) while((s32[]{:T(128)}, f32[4,64,1024]{2,1,0:T(8,128)S(1)}, ...), condition=%wide.region_10.10_spmd, body=%wide.region_9.9_spmd.sunk | while | flops 6292738 | bytes 10583657 | solution.py:75
  354.9 1.5 maximum_dynamic-update-slice_fusion.2
  357.8 1.7 dynamic-slice_bitcast_fusion.3
  359.5 21.7 %while.82 = (s32[]{:T(128)}, f32[4,64,1024]{2,1,0:T(8,128)S(1)}, f32[4,64,1024]{2,1,0:T(8,128)S(1)}, s32[]{:T(128)}, s32[4,64]{1,0:T(4,128)S(1)}, /*index=5*/f32...) while((s32[]{:T(128)}, f32[4,64,1024]{2,1,0:T(8,128)S(1)}, ...), condition=%wide.region_10.10_spmd, body=%wide.region_9.9_spmd.sunk | while | flops 6292738 | bytes 10583657 | solution.py:75
  381.2 1.5 maximum_dynamic-update-slice_fusion.2
  (925 shorter events, 138.0 us)
Async XLA Ops:
  160.9 12.0 %copy-start = (f32[32]{0:T(128)S(1)}, f32[32]{0:T(128)}, u32[]{:S(2)}) copy-start(f32[32]{0:T(128)} %param.12) | copy-start | bytes 388
where the time goes:
time: 388 us; the launch traced here: 383 us
  other arithmetic  131 us (34%)
  loops' own time  111 us (29%)
  local copies, waits for them, and re-layouts  70.2 us (18%)
  blocking collectives  67.4 us (17%)
    select_n x64, other arithmetic, substep(): jnp.where(active, moved_moist - condensed, moist)  91.4 us
    another operation x1, loops' own time, legendre(): lax.scan(legendre_advance, initial, jnp.arange(degrees, dtype=jnp.int32),...  62.2 us
    another operation x8, loops' own time, run_block(): lax.while_loop(unfinished, run_advance, (jnp.int32(0), block_state[0], bl...  48.8 us
    unnamed x1, blocking collectives  33.5 us
    all_gather x1, blocking collectives, shards(): piece = lax.all_gather(filtered, 'lon', axis=0, tiled=True)  30.6 us
    squeeze x8, local copies, waits for them, and re-layouts, run_block(): block_state[1]  13.4 us
    unnamed x4, local copies, waits for them, and re-layouts  13.3 us
    dynamic_update_slice x8, other arithmetic, visit(): return lax.dynamic_update_slice_in_dim(updated, result, start, 1)  11.7 us

commit v1 on v0

v1 whole, which is shorter than its diff:
```python
import jax
import jax.numpy as jnp
from jax import lax
from jax.experimental import pallas as pl
from jax.experimental.pallas import tpu as pltpu
from jax.sharding import PartitionSpec as P

NN = 96
couple_gain = 8.0
LANES = 128
HIGH = lax.Precision.HIGHEST
ALPHA = 0.275


def gather_heating(heating, lon_devices):
    other = lax.ppermute(heating, "lat", [(0, 1), (1, 0)])
    held = jnp.stack([heating, other])[:, None]
    step = 1
    while step < lon_devices:
        pairs = [(i, i ^ step) for i in range(lon_devices)]
        held = jnp.concatenate([held, lax.ppermute(held, "lon", pairs)], 1)
        step *= 2
    return held


def contract(a, b, dims):
    return lax.dot_general(a, b, (dims, ((), ())), precision=HIGH, preferred_element_type=jnp.float32)


def spectral_kernel(where_ref, held_ref, trunc_ref, out_ref, table, partial):
    lon_devices, lon_local, lat_local = held_ref.shape[1:]
    lon_index = where_ref[0]
    lat_index = where_ref[1]
    total_lon = lon_devices * lon_local
    total_lat = 2 * lat_local
    total_modes = where_ref.shape[0] - 2
    modes = lax.broadcasted_iota(jnp.int32, (1, LANES), 1)
    modes_f = modes.astype(jnp.float32)

    row = lax.broadcasted_iota(jnp.int32, (total_lon, LANES), 0)
    lane = lax.broadcasted_iota(jnp.int32, (total_lon, LANES), 1)
    source = (row // lon_local) ^ lon_index
    lon_row = source * lon_local + row % lon_local
    phase = lon_row * lane % total_lon
    angle = phase.astype(jnp.float32) * (2.0 * jnp.pi / total_lon)
    carried = (lane < total_modes).astype(jnp.float32)
    waves = jnp.concatenate([jnp.cos(angle) * carried, jnp.sin(angle) * carried], axis=1)

    rows = (lat_index * lat_local + lax.broadcasted_iota(jnp.int32, (lat_local, 1), 0)).astype(jnp.float32)
    latitude = -0.5 * jnp.pi + jnp.pi * (rows + 0.5) / total_lat
    sin_lat = jnp.broadcast_to(jnp.sin(latitude), (lat_local, LANES))
    cos_lat = jnp.cos(latitude)
    weight = jnp.pi * cos_lat / total_lat / total_lon

    mine = contract(held_ref[0].reshape(total_lon, lat_local), waves, ((0,), (0,)))
    others = contract(held_ref[1].reshape(total_lon, lat_local), waves, ((0,), (0,)))
    r = lax.broadcasted_iota(jnp.int32, (lat_local, lat_local), 0)
    c = lax.broadcasted_iota(jnp.int32, (lat_local, lat_local), 1)
    flip = (r + c == lat_local - 1).astype(jnp.float32)
    others = contract(flip, others, ((1,), (0,)))
    same = (mine + others) * weight
    diff = (mine - others) * weight
    lane2 = lax.broadcasted_iota(jnp.int32, (1, 2 * LANES), 1)
    even_mode = lane2 % 2 == 0
    folded = [jnp.where(even_mode, same, diff), jnp.where(even_mode, diff, same)]

    ladder = (lax.broadcasted_iota(jnp.int32, (NN, LANES), 0) + 1).astype(jnp.float32)
    gains = 0.5 * jnp.log((2.0 * ladder + 1.0) / (2.0 * ladder))
    log_start = 0.5 * jnp.log(jnp.float32(0.5)) + jnp.sum(
        jnp.where(ladder <= modes_f, gains, 0.0), axis=0, keepdims=True
    )
    diagonal = jnp.exp(log_start + modes_f * jnp.log(cos_lat))
    degree = lax.broadcasted_iota(jnp.int32, (NN, LANES), 0).astype(jnp.float32)

    def factor_of(degree_f):
        higher = degree_f > modes_f
        numerator = jnp.maximum(4.0 * degree_f * degree_f - 1.0, 1.0)
        denominator = jnp.where(higher, degree_f * degree_f - modes_f * modes_f, 1.0)
        return higher, jnp.sqrt(numerator / denominator)

    higher, factor = factor_of(degree)
    factor = jnp.where(higher, factor, 0.0)
    below, lower_factor = factor_of(degree - 1.0)
    ratio = jnp.where(below, factor / lower_factor, 0.0)

    previous = jnp.zeros((lat_local, LANES), jnp.float32)
    earlier = jnp.zeros((lat_local, LANES), jnp.float32)
    for n in range(NN):
        raised = factor[n : n + 1] * (sin_lat * previous) - ratio[n : n + 1] * earlier
        current = jnp.where(modes == n, diagonal, raised)
        table[n] = current
        for part in range(2):
            terms = current * folded[n % 2][:, part * LANES : (part + 1) * LANES]
            partial[part, n] = sum(terms[8 * i : 8 * i + 8] for i in range(lat_local // 8))
        previous, earlier = current, previous

    degree_i = lax.broadcasted_iota(jnp.int32, (NN, LANES), 0)
    keep = (degree_i >= modes) & (degree_i <= trunc_ref[0:1, :])
    scale = jnp.where(modes == 0, 1.0, 2.0)
    filtered = []
    for part in range(2):
        spectrum = jnp.where(keep, jnp.sum(partial[part], axis=1) * scale, 0.0)
        total = jnp.zeros((lat_local, LANES), jnp.float32)
        for n in range(NN):
            total = total + table[n] * spectrum[n : n + 1]
        filtered.append(total)
    filtered = jnp.concatenate(filtered, axis=1)
    forcing = contract(filtered, waves[:lon_local], ((1,), (1,)))
    for l in range(lon_local):
        out_ref[l] = jnp.broadcast_to(forcing[:, l : l + 1], (lat_local, LANES))


def cloud_kernel(state_ref, forcing_ref, counts_ref, rate_ref, profile_ref, out_ref):
    lon_block, lat_local, cells = state_ref.shape[1:]
    pieces = cells // LANES
    levels = LANES // 4
    group = 4
    keep_rate = (1.0 - rate_ref[...]) * ALPHA
    move_rate = rate_ref[...] * ALPHA
    lane = lax.broadcasted_iota(jnp.int32, (8, LANES), 1)
    first = lane < levels
    gain = 0.725 / ALPHA
    floor = ALPHA * ALPHA * 0.01

    def body(index, carry):
        columns = []
        for g in range(group):
            row = pl.ds(pl.multiple_of((index * group + g) * 8, 8), 8)
            theta = [state_ref[0, 0, row, pl.ds(LANES * v, LANES)] for v in range(pieces)]
            moist = [state_ref[1, 0, row, pl.ds(LANES * v, LANES)] for v in range(pieces)]
            push = couple_gain * profile_ref[...] * forcing_ref[0, row, :]
            columns.append((row, theta, moist, push, counts_ref[0, row, :]))

        def step(s, carry):
            out = []
            for (row, _, _, push, count), (z, w) in zip(columns, carry):
                active = s < count
                new_z, new_w = [], []
                dry = [x + push for x in z]
                turn_z = [pltpu.roll(x, levels, 1) for x in dry]
                turn_w = [pltpu.roll(x, levels, 1) for x in w]
                for v in range(pieces):
                    back = jnp.where(first, turn_z[v - 1], turn_z[v])
                    new_z.append(jnp.where(active, dry[v] + rate_ref[...] * (back - dry[v]), z[v]))
                    back = jnp.where(first, turn_w[v - 1], turn_w[v])
                    e = keep_rate * w[v] + move_rate * back - (0.2 * ALPHA) * push
                    y = e * e + floor
                    new_w.append(jnp.where(active, gain * e - y * lax.rsqrt(y), w[v]))
                out.append((new_z, new_w))
            return out

        start = [
            ([t + 0.5 * m for t, m in zip(theta, moist)], [m - 0.2 * t - 1.0 for t, m in zip(theta, moist)])
            for _, theta, moist, _, _ in columns
        ]
        most = jnp.max(jnp.maximum(jnp.maximum(columns[0][4], columns[1][4]), jnp.maximum(columns[2][4], columns[3][4])))
        done = lax.fori_loop(0, most, step, start)
        for (row, _, _, _, _), (z, w) in zip(columns, done):
            for v in range(pieces):
                theta = (z[v] - 0.5 * w[v] - 0.5) * (1.0 / 1.1)
                out_ref[0, 0, row, pl.ds(LANES * v, LANES)] = theta
                out_ref[1, 0, row, pl.ds(LANES * v, LANES)] = w[v] + 1.0 + 0.2 * theta
        return carry

    lax.fori_loop(0, lat_local // (8 * group), body, 0)


def shards(cloud_state, counts, courant, truncation):
    lon_devices = lax.axis_size("lon")
    fields, lon_local, lat_local, cells = cloud_state.shape
    levels = courant.shape[0]
    total_modes = truncation.shape[0]
    heating = jnp.mean(cloud_state[0], axis=2)
    held = gather_heating(heating, lon_devices)
    where = jnp.concatenate(
        [jnp.stack([lax.axis_index("lon"), lax.axis_index("lat")]).astype(jnp.int32), jnp.zeros((total_modes,), jnp.int32)]
    )
    trunc = jnp.broadcast_to(jnp.pad(truncation, (0, LANES - total_modes), constant_values=-1)[None], (8, LANES))
    vmem = pl.BlockSpec(memory_space=pltpu.VMEM)
    forcing = pl.pallas_call(
        spectral_kernel,
        in_specs=[pl.BlockSpec(memory_space=pltpu.SMEM), vmem, vmem],
        out_specs=vmem,
        out_shape=jax.ShapeDtypeStruct((lon_local, lat_local, LANES), jnp.float32),
        scratch_shapes=[
            pltpu.VMEM((NN, lat_local, LANES), jnp.float32),
            pltpu.VMEM((2, NN, 8, LANES), jnp.float32),
        ],
        compiler_params=pltpu.CompilerParams(vmem_limit_bytes=48 << 20),
        name="spectral",
    )(where, held, trunc)
    level_profile = jnp.sin(jnp.pi * (jnp.arange(levels).astype(jnp.float32) + 0.5) / levels)
    profile = jnp.tile(level_profile, LANES // levels)[None]
    rate = jnp.tile(courant, LANES // levels)[None]
    count_rows = jnp.broadcast_to(counts[:, :, None], (lon_local, lat_local, LANES))
    state_spec = pl.BlockSpec((fields, 1, lat_local, cells), lambda i: (0, i, 0, 0))
    row_spec = pl.BlockSpec((1, lat_local, LANES), lambda i: (i, 0, 0))
    return pl.pallas_call(
        cloud_kernel,
        grid=(lon_local,),
        in_specs=[state_spec, row_spec, row_spec, vmem, vmem],
        out_specs=state_spec,
        out_shape=jax.ShapeDtypeStruct(cloud_state.shape, jnp.float32),
        name="clouds",
    )(cloud_state, forcing, count_rows, rate, profile)


def solution(mesh):
    return jax.shard_map(
        shards,
        mesh=mesh,
        in_specs=(P("grp", "lon", "lat", None), P(("grp", "lon"), "lat"), P(), P()),
        out_specs=P("grp", "lon", "lat", None),
        check_vma=False,
    )
```

time: 388 us -> 139 us (0.36)
  the two profiles are of different devices: /device:TPU:18 before, /device:TPU:4 now
where the time goes in v1:
time: 139 us; the launch traced here: 140 us
  Pallas kernels  116 us (83%)
  waiting for transfers between devices  10.3 us (7%)
  local copies, waits for them, and re-layouts  5.61 us (4%)
  starting transfers between devices  4.37 us (3%)
  other arithmetic  4 us (3%)
    pallas_call x1, Pallas kernels, shards(): pl.pallas_call(cloud_kernel, grid=(lon_local,), in_specs=[state_spec, row...  112 us
    ppermute x3, waiting for transfers between devices, gather_heating(): held = jnp.concatenate([held, lax.ppermute(held, 'lon', pairs)], 1)  9.08 us
    ppermute x3, starting transfers between devices, gather_heating(): held = jnp.concatenate([held, lax.ppermute(held, 'lon', pairs)], 1)  4.3 us
    pallas_call x1, Pallas kernels, shards(): pl.pallas_call(spectral_kernel, in_specs=[pl.BlockSpec(memory_space=pltpu...  4.04 us
    reduce_sum x1, other arithmetic, shards(): heating = jnp.mean(cloud_state[0], axis=2)  3.82 us
  transfers between devices with their start and end apart: 4, of which 4 were waited for; matrix products, arithmetic and copies ran while one was open for 2% of the time, Pallas kernels for 0%

profile of v1, /device:TPU:4, one launch (start us, length us, event | category | flops | bytes accessed | tf_op | source)
XLA Modules:
  0.0 140.1 jit_solution(12901215190151666077)
XLA Ops:
  0.0 3.8 %slice_reduce_fusion = f32[32,64]{1,0:T(8,128)S(1)} fusion(f32[2,32,64,1024]{3,2,1,0:T(8,128)} %state_ref.1), kind=kLoop, calls=%fused_computation | loop fusion | flops 2095104 | bytes 8396800 | tf_op jit(solution)/shard_map/reduce_sum | solution.py:173
  3.8 0.1 collective-permute-start
  3.9 1.2 collective-permute-done
  5.1 0.0 collective-permute-start.1
  5.1 3.9 %collective-permute-done.1 = f32[2,1,32,64]{3,2,1,0:T(8,128)S(1)} collective-permute-done((f32[2,1,32,64]{3,2,1,0:T(8,128)S(1)}, f32[2,1,32,64]{3,2,1,0:T(8,128)S(1)}, u32[]{:S(2)}, u32[]{:S(2)}) %collective-permute-start.1) | collective-permute-done | bytes 16416 | tf_op jit(solution)/shard_map/ppermute | solution.py:21
  9.0 1.6 %collective-permute-start.2 = (f32[2,2,32,64]{3,2,1,0:T(8,128)S(1)}, f32[2,2,32,64]{3,2,1,0:T(8,128)S(1)}, u32[]{:S(2)}, u32[]{:S(2)}) collective-permute-start(f32[2,2,32,64]{3,2,1,0:T(8,128)S(1)} %pad_maximum_fusion.2), channel_id=1, source_target_pairs={{0,4},{2,6},{4,0},{6,2},{8,12},{10,14},{12,8},{14,10},{1,5},{3,7},... | collective-permute-start | bytes 98312 | tf_op jit(solution)/shard_map/ppermute | solution.py:21
  10.7 0.6 broadcast_in_dim_tile.7.profile_ref
  11.3 0.7 tile.4
  12.0 0.6 broadcast_in_dim_tile.6.rate_ref
  12.6 0.7 pad.4
  13.3 0.1 collective-permute-done.2
  13.4 2.7 %collective-permute-start.3 = (f32[2,4,32,64]{3,2,1,0:T(8,128)S(1)}, f32[2,4,32,64]{3,2,1,0:T(8,128)S(1)}, u32[]{:S(2)}, u32[]{:S(2)}) collective-permute-start(f32[2,4,32,64]{3,2,1,0:T(8,128)S(1)} %pad_maximum_fusion.1), channel_id=1, source_target_pairs={{0,8},{2,10},{4,12},{6,14},{8,0},{10,2},{12,4},{14,6},{1,9},{3,11}... | collective-permute-start | bytes 196616 | tf_op jit(solution)/shard_map/ppermute | solution.py:21
  16.0 0.1 pad_add_fusion.where_ref
  16.1 5.1 %collective-permute-done.3 = f32[2,4,32,64]{3,2,1,0:T(8,128)S(1)} collective-permute-done((f32[2,4,32,64]{3,2,1,0:T(8,128)S(1)}, f32[2,4,32,64]{3,2,1,0:T(8,128)S(1)}, u32[]{:S(2)}, u32[]{:S(2)}) %collective-permute-start.3) | collective-permute-done | bytes 65568 | tf_op jit(solution)/shard_map/ppermute | solution.py:21
  21.3 4.0 %spectral.1.forcing_ref = f32[32,64,128]{2,1,0:T(8,128)S(1)} custom-call(s32[98]{0:T(128)S(1)} %pad_add_fusion.where_ref, f32[2,8,32,64]{3,2,1,0:T(8,128)S(1)} %pad_maximum_fusion.held_ref, s32[8,128]{1,0:T(8,128)S(1)} %broadcast_in_dim.20.trunc_ref), custom_call_target="tpu_custom_call" | custom-call | tf_op jit(solution)/shard_map/spectral/pallas_call | solution.py:180
  25.3 0.0 copy-start
  25.3 1.0 copy-done
  26.3 2.1 %broadcast_in_dim.21.counts_ref = s32[32,64,128]{2,1,0:T(8,128)} broadcast(s32[32,64]{1,0:T(8,128)} %param.5), dimensions={0,1} | broadcast | bytes 1056768 | tf_op jit(solution)/shard_map/broadcast_in_dim | solution.py:195
  28.3 111.7 %clouds.1 = f32[2,32,64,1024]{3,2,1,0:T(8,128)} custom-call(f32[2,32,64,1024]{3,2,1,0:T(8,128)} %state_ref.1, f32[32,64,128]{2,1,0:T(8,128)} %copy-done, s32[32,64,128]{2,1,0:T(8,128)} %broadcast_in_dim.21.counts_ref, f32[1,128]{1,0:T(1,128)} %broadcast_in_dim_tile.6.rate_ref, f32[1,128]{1,0:T(1,128)} %broadcast_in_dim_tile.7.profile_ref), custom_call_target="tpu_custom_call" | custom-call | tf_op jit(solution)/shard_map/clouds/pallas_call | solution.py:198
  (9 shorter events, 0.1 us)
Async XLA Ops:
  3.8 1.2 collective-permute-start
  5.1 3.9 %collective-permute-start.1 = (f32[2,1,32,64]{3,2,1,0:T(8,128)S(1)}, f32[2,1,32,64]{3,2,1,0:T(8,128)S(1)}, u32[]{:S(2)}, u32[]{:S(2)}) collective-permute-start(f32[2,1,32,64]{3,2,1,0:T(8,128)S(1)} %maximum_bitcast_fusion), channel_id=1, source_target_pairs={{0,2},{2,0},{4,6},{6,4},{8,10},{10,8},{12,14},{14,12},{1,3},{3,1},... | collective-permute-start | bytes 49160 | tf_op jit(solution)/shard_map/ppermute | solution.py:21
  9.0 4.3 %collective-permute-start.2 = (f32[2,2,32,64]{3,2,1,0:T(8,128)S(1)}, f32[2,2,32,64]{3,2,1,0:T(8,128)S(1)}, u32[]{:S(2)}, u32[]{:S(2)}) collective-permute-start(f32[2,2,32,64]{3,2,1,0:T(8,128)S(1)} %pad_maximum_fusion.2), channel_id=1, source_target_pairs={{0,4},{2,6},{4,0},{6,2},{8,12},{10,14},{12,8},{14,10},{1,5},{3,7},... | collective-permute-start | bytes 98312 | tf_op jit(solution)/shard_map/ppermute | solution.py:21
  13.4 7.9 %collective-permute-start.3 = (f32[2,4,32,64]{3,2,1,0:T(8,128)S(1)}, f32[2,4,32,64]{3,2,1,0:T(8,128)S(1)}, u32[]{:S(2)}, u32[]{:S(2)}) collective-permute-start(f32[2,4,32,64]{3,2,1,0:T(8,128)S(1)} %pad_maximum_fusion.1), channel_id=1, source_target_pairs={{0,8},{2,10},{4,12},{6,14},{8,0},{10,2},{12,4},{14,6},{1,9},{3,11}... | collective-permute-start | bytes 196616 | tf_op jit(solution)/shard_map/ppermute | solution.py:21
  25.3 1.0 copy-start
